TPU v7x, 32 devices: a whole 2x2x4 slice. The times are simulated.
32 devices in a mesh: slab: 8 (over z, y), sub: 4 (over x, core).
Axes of the slice: x: 2, y: 2, z: 4, core: 2. Of those that a mesh axis runs over, the one named last changes fastest.
Arguments:
- coefficients: bfloat16 [7, 6, 6, 64, 12, 128], P(None, None, None, 'slab', 'sub'), may hold values from -1 to 1
- earlier: float32 [30, 6, 64, 12, 128], P(None, None, 'slab', 'sub'), may hold values from -6 to 6
- start: float32 [6, 64, 12, 128], P(None, 'slab', 'sub'), may hold values from -8 to 8
- shifts: float32 [5], replicated, may hold values from -0.3 to 0.3
Outputs:
- new_basis: float32 [6, 6, 64, 12, 128], P(None, None, 'slab', 'sub')
- projection: float32 [30, 6], replicated
- triangle: float32 [6, 6], replicated
All inputs are finite; a program needn't handle non-finite values.
Results may differ from a plain program's by a relative error of at most 0.0015.
Values may be sent and summed in bfloat16 or wider, within the bound.
A program may use at most 64 MiB of HBM per device.

v0:
```python
import jax
import jax.numpy as jnp
from jax import lax
from jax.sharding import PartitionSpec as P


def padded_2(block, sides, width):
    for axis, dim in sides:
        count = lax.axis_size(axis)
        forward = [(i, i + 1) for i in range(count - 1)]
        backward = [(target, source) for source, target in forward]
        low = lax.ppermute(
            lax.slice_in_dim(block, block.shape[dim] - width, None, axis=dim), axis, forward
        )
        high = lax.ppermute(lax.slice_in_dim(block, 0, width, axis=dim), axis, backward)
        block = jnp.concatenate([low, block, high], axis=dim)
    return block


def nearby_fields(padded):
    center = padded[:, 1:-1, 1:-1]
    zeros_edge = jnp.zeros_like(center[..., :1])
    lower_y = jnp.concatenate([zeros_edge, center[..., :-1]], axis=3)
    upper_y = jnp.concatenate([center[..., 1:], zeros_edge], axis=3)
    return [
        center,
        padded[:, :-2, 1:-1],
        padded[:, 2:, 1:-1],
        padded[:, 1:-1, :-2],
        padded[:, 1:-1, 2:],
        lower_y,
        upper_y,
    ]


def apply_padded(coefficients, padded, theta):
    fields = nearby_fields(padded)
    result = (1.0 - theta) * fields[0]
    for coupling in range(len(fields)):
        result = result + jnp.sum(coefficients[coupling] * fields[coupling][None], axis=1)
    return result


def body(coefficients, earlier, start, shifts):
    depth = shifts.shape[0]
    vectors = [start]
    current = padded_2(start, (("slab", 1),), depth)
    wide_coefficients = padded_2(coefficients, (("slab", 3),), depth)
    for step in range(depth):
        beside = padded_2(current, (("sub", 2),), 1)
        padded = jnp.pad(beside, ((0, 0), (1, 1), (0, 0), (0, 0)))
        current = apply_padded(wide_coefficients, padded, shifts[step])
        vectors.append(current[:, depth:-depth])
    basis = jnp.stack(vectors)
    block_count = basis.shape[0]
    flat = basis.reshape(block_count, -1)
    earlier_flat = earlier.reshape(earlier.shape[0], -1)
    count = flat.shape[1] * lax.axis_size("slab") * lax.axis_size("sub")
    local_cross = jnp.dot(earlier_flat, flat.T, precision=lax.Precision.HIGHEST)
    local_self = jnp.dot(flat, flat.T, precision=lax.Precision.HIGHEST)
    local_earlier = jnp.dot(earlier_flat, earlier_flat.T, precision=lax.Precision.HIGHEST)
    cross_sum, self_sum, earlier_sum = lax.psum(
        (local_cross, local_self, local_earlier), ("slab", "sub")
    )
    projection = cross_sum / count
    rest = flat - jnp.dot(projection.T, earlier_flat, precision=lax.Precision.HIGHEST)
    weighted = jnp.dot(earlier_sum / count, projection, precision=lax.Precision.HIGHEST)
    gram = self_sum / count - 2.0 * jnp.dot(
        projection.T, projection, precision=lax.Precision.HIGHEST
    )
    gram = gram + jnp.dot(projection.T, weighted, precision=lax.Precision.HIGHEST)
    lower = jnp.linalg.cholesky(gram)
    new_flat = lax.linalg.triangular_solve(lower, rest, left_side=True, lower=True)
    return (new_flat.reshape(basis.shape), projection, lower.T)


def solution(mesh):
    placed = (
        P(None, None, None, "slab", "sub", None),
        P(None, None, "slab", "sub", None),
        P(None, "slab", "sub", None),
        P(),
    )
    return jax.shard_map(
        body,
        mesh=mesh,
        in_specs=placed,
        out_specs=(P(None, None, "slab", "sub", None), P(), P()),
        check_vma=False,
    )
```

profile of v0, /device:TPU:0, one launch (start us, length us, event | category | flops | bytes accessed | tf_op | source)
XLA Modules:
  0.0 177.3 jit_solution(12425602278455781404)
XLA Ops:
  0.6 1.0 fusion.71
  1.6 1.3 collective-permute-start.1
  2.9 5.5 %collective-permute-start = (f32[6,5,3,128]{3,1,2,0:T(8,128)S(1)}, f32[6,5,3,128]{3,1,2,0:T(8,128)S(1)}, u32[]{:S(2)}, u32[]{:S(2)}) collective-permute-start(f32[6,5,3,128]{3,1,2,0:T(8,128)S(1)} %get-tuple-element.112), channel_id=1, source_target_pairs={{0,4},{4,8},{8,12},{12,16},{16,20},{20,24},{24,28},{1,5},{5,9},{9,... | collective-permute-start | bytes 138248 | tf_op jit(solution)/shard_map/ppermute | solution.py:12
  8.4 2.5 %fusion.55 = (bf16[7,6,6,5,3,128]{5,3,4,2,1,0:T(8,128)(2,1)S(1)}, bf16[7,6,6,5,3,128]{5,3,4,2,1,0:T(8,128)(2,1)S(1)}) fusion(bf16[7,6,6,8,3,128]{5,3,4,2,1,0:T(8,128)(2,1)} %param.4), kind=kLoop, calls=%fused_computation.150 | loop fusion | bytes 3870720 | tf_op jit(solution)/shard_map/slice | solution.py:13
  10.9 1.5 copy.352
  12.4 1.3 collective-permute-start.3
  13.7 1.5 copy.351
  15.2 6.6 %collective-permute-start.2 = (bf16[7,6,6,5,3,128]{5,0,4,3,2,1:T(8,128)(2,1)}, bf16[7,6,6,5,3,128]{5,0,4,3,2,1:T(8,128)(2,1)}, u32[]{:S(2)}, u32[]{:S(2)}) collective-permute-start(bf16[7,6,6,5,3,128]{5,0,4,3,2,1:T(8,128)(2,1)} %copy.351), channel_id=1, source_target_pairs={{0,4},{4,8},{8,12},{12,16},{16,20},{20,24},{24,28},{1,5},{5,9},{9,... | collective-permute-start | bytes 2903048 | tf_op jit(solution)/shard_map/ppermute | solution.py:12
  21.8 2.3 %fusion.39 = f32[30,30]{1,0:T(8,128)S(1)} fusion(f32[30,6,8,3,128]{4,2,3,1,0:T(8,128)S(1)} %copy-done.1), kind=kOutput, calls=%fused_computation.76 | convolution fusion | flops 199065600 | bytes 2215440 | tf_op jit(solution)/shard_map/dot_general | solution.py:61
  24.1 0.7 fusion.72
  24.9 2.6 %copy.340 = f32[30,6,8,3,128]{4,3,2,1,0:T(4,128)} copy(f32[30,6,8,3,128]{4,2,3,1,0:T(8,128)S(1)} %copy-done.1) | data formatting | bytes 4423680 | tf_op args[1]
  30.8 4.5 %reshape.317 = f32[30,18432]{1,0:T(8,128)} reshape(f32[30,6,8,3,128]{4,3,2,1,0:T(4,128)} %copy.340) | data formatting | bytes 4423680 | tf_op jit(solution)/shard_map/reshape | solution.py:57
  35.4 1.3 collective-permute-start.4
  36.7 1.3 collective-permute-start.5
  38.3 3.3 %collective-permute-done.5 = f32[6,18,1,128]{3,1,2,0:T(8,128)S(1)} collective-permute-done((f32[6,18,1,128]{3,1,2,0:T(8,128)S(1)}, f32[6,18,1,128]{3,1,2,0:T(8,128)S(1)}, u32[]{:S(2)}, u32[]{:S(2)}) %collective-permute-start.5) | collective-permute-done | bytes 55328 | tf_op jit(solution)/shard_map/ppermute | solution.py:15
  41.7 1.6 copy.319
  43.3 21.9 %collective-permute-done.2 = bf16[7,6,6,5,3,128]{5,0,4,3,2,1:T(8,128)(2,1)} collective-permute-done((bf16[7,6,6,5,3,128]{5,0,4,3,2,1:T(8,128)(2,1)}, bf16[7,6,6,5,3,128]{5,0,4,3,2,1:T(8,128)(2,1)}, u32[]{:S(2)}, u32[]{:S(2)}) %collective-permute-start.2) | collective-permute-done | bytes 967712 | tf_op jit(solution)/shard_map/ppermute | solution.py:12
  65.2 1.6 copy.318
  66.8 2.9 %pad_maximum_fusion = bf16[7,6,6,18,3,128]{5,3,4,2,1,0:T(8,128)(2,1)S(1)} fusion(bf16[7,6,6,5,3,128]{5,3,4,2,1,0:T(8,128)(2,1)S(1)} %copy.319, bf16[7,6,6,8,3,128]{5,3,4,2,1,0:T(8,128)(2,1)S(1)} %copy-done.2, bf16[7,6,6,5,3,128]{5,3,4,2,1,0:T(8,128)(2,1)S(1)} %copy.318), kind=kLoop, calls=%fused_computation.1 | loop fusion | flops 10450944 | bytes 6967296 | tf_op jit(solution)/shard_map/concatenate | solution.py:16
  69.7 1.1 fusion.4
  70.8 1.1 copy-done
  71.9 0.1 add_add_fusion.3
  72.1 0.6 fusion.67
  72.8 1.9 %collective-permute-start.6 = (f32[6,18,1,128]{3,1,2,0:T(8,128)}, f32[6,18,1,128]{3,1,2,0:T(8,128)S(1)}, u32[]{:S(2)}, u32[]{:S(2)}) collective-permute-start(f32[6,18,1,128]{3,1,2,0:T(8,128)} %get-tuple-element.102), channel_id=1, source_target_pairs={{0,1},{1,2},{2,3},{4,5},{5,6},{6,7},{8,9},{9,10},{10,11},{12,13},{... | collective-permute-start | bytes 165896 | tf_op jit(solution)/shard_map/ppermute | solution.py:12
  74.7 1.5 collective-permute-start.7
  76.2 0.7 stack.43
  77.2 1.7 collective-permute-done.7
  79.1 3.5 %fusion.5 = (f32[6,18,3,128]{3,1,2,0:T(8,128)S(1)}, f32[6,18,3,128]{3,1,2,0:T(8,128)S(1)}, f32[6,18,3,128]{3,1,2,0:T(8,128)S(1)}, f32[6,18,3,128]{3,1,2,0:T(8,12...) fusion(f32[6,18,3,128]{3,1,2,0:T(8,128)S(1)} %add_add_fusion.3, ...), kind=kLoop, calls=%fused_computation.42 | loop fusion | flops 4935168 | bytes 5806080 | tf_op jit(solution)/shard_map/reduce_sum | solution.py:40
  82.8 0.7 fusion.65
  83.5 4.9 %collective-permute-start.8 = (f32[6,18,1,128]{3,1,2,0:T(8,128)}, f32[6,18,1,128]{3,1,2,0:T(8,128)S(1)}, u32[]{:S(2)}, u32[]{:S(2)}) collective-permute-start(f32[6,18,1,128]{3,1,2,0:T(8,128)} %get-tuple-element.96), channel_id=1, source_target_pairs={{0,1},{1,2},{2,3},{4,5},{5,6},{6,7},{8,9},{9,10},{10,11},{12,13},{... | collective-permute-start | bytes 165896 | tf_op jit(solution)/shard_map/ppermute | solution.py:12
  88.4 1.3 collective-permute-start.9
  89.8 0.7 stack.44
  90.7 1.0 collective-permute-done.9
  91.9 3.5 %fusion.6 = (f32[6,18,3,128]{3,1,2,0:T(8,128)S(1)}, f32[6,18,3,128]{3,1,2,0:T(8,128)S(1)}, f32[6,18,3,128]{3,1,2,0:T(8,128)S(1)}, f32[6,18,3,128]{3,1,2,0:T(8,12...) fusion(f32[6,18,3,128]{3,1,2,0:T(8,128)S(1)} %add_add_fusion.2, ...), kind=kLoop, calls=%fused_computation.43 | loop fusion | flops 4935168 | bytes 5806080 | tf_op jit(solution)/shard_map/reduce_sum | solution.py:40
  95.7 0.7 fusion.63
  96.4 4.4 %collective-permute-start.10 = (f32[6,18,1,128]{3,1,2,0:T(8,128)}, f32[6,18,1,128]{3,1,2,0:T(8,128)S(1)}, u32[]{:S(2)}, u32[]{:S(2)}) collective-permute-start(f32[6,18,1,128]{3,1,2,0:T(8,128)} %get-tuple-element.90), channel_id=1, source_target_pairs={{0,1},{1,2},{2,3},{4,5},{5,6},{6,7},{8,9},{9,10},{10,11},{12,13},{... | collective-permute-start | bytes 165896 | tf_op jit(solution)/shard_map/ppermute | solution.py:12
  100.8 1.3 collective-permute-start.11
  102.1 0.6 slice_bitcast_fusion.8
  102.8 0.7 stack.45
  103.7 1.0 copy.323
  104.8 3.5 %fusion.7 = (f32[6,18,3,128]{3,1,2,0:T(8,128)S(1)}, f32[6,18,3,128]{3,1,2,0:T(8,128)S(1)}, f32[6,18,3,128]{3,1,2,0:T(8,128)S(1)}, f32[6,18,3,128]{3,1,2,0:T(8,12...) fusion(f32[6,18,3,128]{3,1,2,0:T(8,128)S(1)} %add_add_fusion.1, ...), kind=kLoop, calls=%fused_computation.44 | loop fusion | flops 4935168 | bytes 5806080 | tf_op jit(solution)/shard_map/reduce_sum | solution.py:40
  108.6 0.7 fusion.61
  109.3 4.0 %collective-permute-start.12 = (f32[6,18,1,128]{3,1,2,0:T(8,128)}, f32[6,18,1,128]{3,1,2,0:T(8,128)S(1)}, u32[]{:S(2)}, u32[]{:S(2)}) collective-permute-start(f32[6,18,1,128]{3,1,2,0:T(8,128)} %get-tuple-element.84), channel_id=1, source_target_pairs={{0,1},{1,2},{2,3},{4,5},{5,6},{6,7},{8,9},{9,10},{10,11},{12,13},{... | collective-permute-start | bytes 165896 | tf_op jit(solution)/shard_map/ppermute | solution.py:12
  113.3 1.3 collective-permute-start.13
  114.6 0.6 slice_bitcast_fusion.7
  115.2 0.7 stack.46
  116.1 1.0 copy.324
  117.2 3.5 %fusion.8 = (f32[6,18,3,128]{3,1,2,0:T(8,128)S(1)}, f32[6,18,3,128]{3,1,2,0:T(8,128)S(1)}, f32[6,18,3,128]{3,1,2,0:T(8,128)S(1)}, f32[6,18,3,128]{3,1,2,0:T(8,12...) fusion(f32[6,18,3,128]{3,1,2,0:T(8,128)S(1)} %add_add_fusion, ...), kind=kLoop, calls=%fused_computation.45 | loop fusion | flops 4935168 | bytes 5806080 | tf_op jit(solution)/shard_map/reduce_sum | solution.py:40
  121.0 0.7 stack.41
  121.8 2.2 %fusion.42 = f32[30,6]{0,1:T(8,128)S(1)} fusion(f32[6,6,8,3,128]{4,0,3,2,1:T(8,128)S(1)} %stack.41, f32[30,6,8,3,128]{4,2,3,1,0:T(8,128)S(1)} %copy-done.1), kind=kOutput, calls=%fused_computation.77 | convolution fusion | flops 39813120 | bytes 2654928 | tf_op jit(solution)/shard_map/dot_general | solution.py:59
  124.0 1.4 convolution_bitcast_fusion
  125.5 42.9 %all-reduce.15 = (f32[30,6]{0,1:T(8,128)S(1)}, f32[6,6]{0,1:T(8,128)S(1)}, f32[30,30]{1,0:T(8,128)S(1)}) all-reduce(f32[30,6]{0,1:T(8,128)S(1)} %fusion.42, f32[6,6]{0,1:T(8,128)S(1)} %convolution_bitcast_fusion, f32[30,30]{1,0:T(8,128)S(1)} %fusion.39), channel_id=1, replica_groups=mesh['slab'=8,'sub'=4] {'slab','sub'}, use_global_device_ids=true, to_apply=%region_36.37 | all-reduce | flops 1116 | bytes 8928 | tf_op jit(solution)/shard_map/psum | solution.py:62
  168.4 0.1 fusion.45
  168.6 0.1 fusion.47
  168.7 0.1 convolution_add_fusion
  169.0 0.5 cholesky.16
  169.5 0.6 compare_reduce_fusion
  170.2 0.6 fusion.53
  170.8 0.5 custom-call.6
  171.3 0.7 stack.48
  172.1 2.9 %convolution_subtract_fusion = f32[6,18432]{1,0:T(8,128)S(1)} fusion(f32[6,18432]{1,0:T(8,128)S(1)} %stack.48, f32[30,6]{0,1:T(8,128)S(1)} %broadcast_multiply_fusion, f32[30,18432]{1,0:T(8,128)} %reshape.317), kind=kOutput, calls=%fused_computation | convolution fusion | flops 39923712 | bytes 3097296 | tf_op jit(solution)/shard_map/dot_general | solution.py:66
  175.0 0.8 fusion.50
  175.7 0.8 copy.342
  176.6 0.7 copy.343
  (83 shorter events, 3.3 us)
Async XLA Ops:
  1.6 33.7 %collective-permute-start.1 = (f32[6,5,3,128]{3,1,2,0:T(8,128)S(1)}, f32[6,5,3,128]{3,1,2,0:T(8,128)S(1)}, u32[]{:S(2)}, u32[]{:S(2)}) collective-permute-start(f32[6,5,3,128]{3,1,2,0:T(8,128)S(1)} %get-tuple-element.113), channel_id=1, source_target_pairs={{4,0},{8,4},{12,8},{16,12},{20,16},{24,20},{28,24},{5,1},{9,5},{13... | collective-permute-start | bytes 138248 | tf_op jit(solution)/shard_map/ppermute | solution.py:15
  2.9 32.4 %collective-permute-start = (f32[6,5,3,128]{3,1,2,0:T(8,128)S(1)}, f32[6,5,3,128]{3,1,2,0:T(8,128)S(1)}, u32[]{:S(2)}, u32[]{:S(2)}) collective-permute-start(f32[6,5,3,128]{3,1,2,0:T(8,128)S(1)} %get-tuple-element.112), channel_id=1, source_target_pairs={{0,4},{4,8},{8,12},{12,16},{16,20},{20,24},{24,28},{1,5},{5,9},{9,... | collective-permute-start | bytes 138248 | tf_op jit(solution)/shard_map/ppermute | solution.py:12
  12.4 29.3 %collective-permute-start.3 = (bf16[7,6,6,5,3,128]{5,0,4,3,2,1:T(8,128)(2,1)}, bf16[7,6,6,5,3,128]{5,0,4,3,2,1:T(8,128)(2,1)}, u32[]{:S(2)}, u32[]{:S(2)}) collective-permute-start(bf16[7,6,6,5,3,128]{5,0,4,3,2,1:T(8,128)(2,1)} %copy.352), channel_id=1, source_target_pairs={{4,0},{8,4},{12,8},{16,12},{20,16},{24,20},{28,24},{5,1},{9,5},{13... | collective-permute-start | bytes 2903048 | tf_op jit(solution)/shard_map/ppermute | solution.py:15
  13.7 8.1 %copy-start.1 = (f32[30,6,8,3,128]{4,2,3,1,0:T(8,128)S(1)}, f32[30,6,8,3,128]{4,2,3,1,0:T(8,128)}, u32[]{:S(2)}) copy-start(f32[30,6,8,3,128]{4,2,3,1,0:T(8,128)} %param.5) | copy-start | bytes 6635524
  15.2 8.9 %copy-start.9 = (f32[5]{0:T(128)S(1)}, f32[5]{0:T(128)}, u32[]{:S(2)}) copy-start(f32[5]{0:T(128)} %param.7) | copy-start | bytes 64
  15.2 9.6 %copy-start.3 = (f32[6,8,3,128]{3,1,2,0:T(8,128)S(1)}, f32[6,8,3,128]{3,1,2,0:T(8,128)}, u32[]{:S(2)}) copy-start(f32[6,8,3,128]{3,1,2,0:T(8,128)} %param.6) | copy-start | bytes 221188
  15.2 50.0 %collective-permute-start.2 = (bf16[7,6,6,5,3,128]{5,0,4,3,2,1:T(8,128)(2,1)}, bf16[7,6,6,5,3,128]{5,0,4,3,2,1:T(8,128)(2,1)}, u32[]{:S(2)}, u32[]{:S(2)}) collective-permute-start(bf16[7,6,6,5,3,128]{5,0,4,3,2,1:T(8,128)(2,1)} %copy.351), channel_id=1, source_target_pairs={{0,4},{4,8},{8,12},{12,16},{16,20},{20,24},{24,28},{1,5},{5,9},{9,... | collective-permute-start | bytes 2903048 | tf_op jit(solution)/shard_map/ppermute | solution.py:12
  35.4 2.9 %collective-permute-start.4 = (f32[6,18,1,128]{3,1,2,0:T(8,128)S(1)}, f32[6,18,1,128]{3,1,2,0:T(8,128)S(1)}, u32[]{:S(2)}, u32[]{:S(2)}) collective-permute-start(f32[6,18,1,128]{3,1,2,0:T(8,128)S(1)} %get-tuple-element.108), channel_id=1, source_target_pairs={{0,1},{1,2},{2,3},{4,5},{5,6},{6,7},{8,9},{9,10},{10,11},{12,13},{... | collective-permute-start | bytes 165896 | tf_op jit(solution)/shard_map/ppermute | solution.py:12
  36.7 4.9 %collective-permute-start.5 = (f32[6,18,1,128]{3,1,2,0:T(8,128)S(1)}, f32[6,18,1,128]{3,1,2,0:T(8,128)S(1)}, u32[]{:S(2)}, u32[]{:S(2)}) collective-permute-start(f32[6,18,1,128]{3,1,2,0:T(8,128)S(1)} %get-tuple-element.109), channel_id=1, source_target_pairs={{1,0},{2,1},{3,2},{5,4},{6,5},{7,6},{9,8},{10,9},{11,10},{13,12},{... | collective-permute-start | bytes 165896 | tf_op jit(solution)/shard_map/ppermute | solution.py:15
  43.3 23.5 %copy-start.2 = (bf16[7,6,6,8,3,128]{5,3,4,2,1,0:T(8,128)(2,1)S(1)}, bf16[7,6,6,8,3,128]{5,3,4,2,1,0:T(8,128)(2,1)}, u32[]{:S(2)}) copy-start(bf16[7,6,6,8,3,128]{5,3,4,2,1,0:T(8,128)(2,1)} %param.4) | copy-start | bytes 4644868
  69.7 2.2 %copy-start = (bf16[7,6,6,18,3,128]{5,3,4,2,1,0:T(8,128)(2,1)}, bf16[7,6,6,18,3,128]{5,3,4,2,1,0:T(8,128)(2,1)S(1)}, u32[]{:S(2)}) copy-start(bf16[7,6,6,18,3,128]{5,3,4,2,1,0:T(8,128)(2,1)S(1)} %pad_maximum_fusion) | copy-start | bytes 10450948
  72.8 4.4 %collective-permute-start.6 = (f32[6,18,1,128]{3,1,2,0:T(8,128)}, f32[6,18,1,128]{3,1,2,0:T(8,128)S(1)}, u32[]{:S(2)}, u32[]{:S(2)}) collective-permute-start(f32[6,18,1,128]{3,1,2,0:T(8,128)} %get-tuple-element.102), channel_id=1, source_target_pairs={{0,1},{1,2},{2,3},{4,5},{5,6},{6,7},{8,9},{9,10},{10,11},{12,13},{... | collective-permute-start | bytes 165896 | tf_op jit(solution)/shard_map/ppermute | solution.py:12
  74.7 4.3 %collective-permute-start.7 = (f32[6,18,1,128]{3,1,2,0:T(8,128)S(1)}, f32[6,18,1,128]{3,1,2,0:T(8,128)S(1)}, u32[]{:S(2)}, u32[]{:S(2)}) collective-permute-start(f32[6,18,1,128]{3,1,2,0:T(8,128)S(1)} %get-tuple-element.103), channel_id=1, source_target_pairs={{1,0},{2,1},{3,2},{5,4},{6,5},{7,6},{9,8},{10,9},{11,10},{13,12},{... | collective-permute-start | bytes 165896 | tf_op jit(solution)/shard_map/ppermute | solution.py:15
  83.5 7.2 %collective-permute-start.8 = (f32[6,18,1,128]{3,1,2,0:T(8,128)}, f32[6,18,1,128]{3,1,2,0:T(8,128)S(1)}, u32[]{:S(2)}, u32[]{:S(2)}) collective-permute-start(f32[6,18,1,128]{3,1,2,0:T(8,128)} %get-tuple-element.96), channel_id=1, source_target_pairs={{0,1},{1,2},{2,3},{4,5},{5,6},{6,7},{8,9},{9,10},{10,11},{12,13},{... | collective-permute-start | bytes 165896 | tf_op jit(solution)/shard_map/ppermute | solution.py:12
  88.4 3.4 %collective-permute-start.9 = (f32[6,18,1,128]{3,1,2,0:T(8,128)}, f32[6,18,1,128]{3,1,2,0:T(8,128)S(1)}, u32[]{:S(2)}, u32[]{:S(2)}) collective-permute-start(f32[6,18,1,128]{3,1,2,0:T(8,128)} %get-tuple-element.97), channel_id=1, source_target_pairs={{1,0},{2,1},{3,2},{5,4},{6,5},{7,6},{9,8},{10,9},{11,10},{13,12},{... | collective-permute-start | bytes 165896 | tf_op jit(solution)/shard_map/ppermute | solution.py:15
  96.4 8.2 %collective-permute-start.10 = (f32[6,18,1,128]{3,1,2,0:T(8,128)}, f32[6,18,1,128]{3,1,2,0:T(8,128)S(1)}, u32[]{:S(2)}, u32[]{:S(2)}) collective-permute-start(f32[6,18,1,128]{3,1,2,0:T(8,128)} %get-tuple-element.90), channel_id=1, source_target_pairs={{0,1},{1,2},{2,3},{4,5},{5,6},{6,7},{8,9},{9,10},{10,11},{12,13},{... | collective-permute-start | bytes 165896 | tf_op jit(solution)/shard_map/ppermute | solution.py:12
  100.8 3.8 %collective-permute-start.11 = (f32[6,18,1,128]{3,1,2,0:T(8,128)}, f32[6,18,1,128]{3,1,2,0:T(8,128)S(1)}, u32[]{:S(2)}, u32[]{:S(2)}) collective-permute-start(f32[6,18,1,128]{3,1,2,0:T(8,128)} %get-tuple-element.91), channel_id=1, source_target_pairs={{1,0},{2,1},{3,2},{5,4},{6,5},{7,6},{9,8},{10,9},{11,10},{13,12},{... | collective-permute-start | bytes 165896 | tf_op jit(solution)/shard_map/ppermute | solution.py:15
  109.3 7.8 %collective-permute-start.12 = (f32[6,18,1,128]{3,1,2,0:T(8,128)}, f32[6,18,1,128]{3,1,2,0:T(8,128)S(1)}, u32[]{:S(2)}, u32[]{:S(2)}) collective-permute-start(f32[6,18,1,128]{3,1,2,0:T(8,128)} %get-tuple-element.84), channel_id=1, source_target_pairs={{0,1},{1,2},{2,3},{4,5},{5,6},{6,7},{8,9},{9,10},{10,11},{12,13},{... | collective-permute-start | bytes 165896 | tf_op jit(solution)/shard_map/ppermute | solution.py:12
  113.3 3.8 %collective-permute-start.13 = (f32[6,18,1,128]{3,1,2,0:T(8,128)}, f32[6,18,1,128]{3,1,2,0:T(8,128)S(1)}, u32[]{:S(2)}, u32[]{:S(2)}) collective-permute-start(f32[6,18,1,128]{3,1,2,0:T(8,128)} %get-tuple-element.85), channel_id=1, source_target_pairs={{1,0},{2,1},{3,2},{5,4},{6,5},{7,6},{9,8},{10,9},{11,10},{13,12},{... | collective-permute-start | bytes 165896 | tf_op jit(solution)/shard_map/ppermute | solution.py:15
  124.0 47.3 %copy-start.4 = (f32[1,18432]{1,0:T(1,128)S(1)}, f32[1,18432]{1,0:T(1,128)}, u32[]{:S(2)}) copy-start(f32[1,18432]{1,0:T(1,128)} %stack.43) | copy-start | bytes 221188
  124.0 47.3 %copy-start.5 = (f32[1,18432]{1,0:T(1,128)S(1)}, f32[1,18432]{1,0:T(1,128)}, u32[]{:S(2)}) copy-start(f32[1,18432]{1,0:T(1,128)} %stack.44) | copy-start | bytes 221188
  124.0 47.3 %copy-start.6 = (f32[1,18432]{1,0:T(1,128)S(1)}, f32[1,18432]{1,0:T(1,128)}, u32[]{:S(2)}) copy-start(f32[1,18432]{1,0:T(1,128)} %stack.45) | copy-start | bytes 221188
  124.0 47.3 %copy-start.7 = (f32[1,18432]{1,0:T(1,128)S(1)}, f32[1,18432]{1,0:T(1,128)}, u32[]{:S(2)}) copy-start(f32[1,18432]{1,0:T(1,128)} %stack.46) | copy-start | bytes 221188
  168.4 6.5 %copy-start.8 = (f32[30,6]{0,1:T(8,128)}, f32[30,6]{0,1:T(8,128)S(1)}, u32[]{:S(2)}) copy-start(f32[30,6]{0,1:T(8,128)S(1)} %broadcast_multiply_fusion) | copy-start | bytes 2164
where the time goes:
time: 178 us; the launch traced here: 177 us
  blocking collectives  42.9 us (24%)
  starting transfers between devices  37.9 us (21%)
  local copies, waits for them, and re-layouts  32.4 us (18%)
  waiting for transfers between devices  28 us (16%)
  other arithmetic  21.6 us (12%)
  matrix products  9.97 us (6%)
  between operations  4.5 us (3%)
    psum x1, blocking collectives, body(): lax.psum((local_cross, local_self, local_earlier), ('slab', 'sub'))  42.9 us
    ppermute x7, starting transfers between devices, padded_2(): lax.ppermute(lax.slice_in_dim(block, block.shape[dim] - width, None, axis...  28.7 us
    ppermute x7, waiting for transfers between devices, padded_2(): lax.ppermute(lax.slice_in_dim(block, block.shape[dim] - width, None, axis...  21.9 us
    reduce_sum x5, other arithmetic, apply_padded(): jnp.sum(coefficients[coupling] * fields[coupling][None], axis=1)  15.2 us
    ppermute x7, starting transfers between devices, padded_2(): lax.ppermute(lax.slice_in_dim(block, 0, width, axis=dim), axis, backward)  9.21 us
    unnamed x26, local copies, waits for them, and re-layouts  8.24 us
    another operation x18, local copies, waits for them, and re-layouts, body(): basis = jnp.stack(vectors)  8.1 us
    slice x7, local copies, waits for them, and re-layouts, padded_2(): lax.slice_in_dim(block, block.shape[dim] - width, None, axis=dim)  6.15 us
  transfers between devices with their start and end apart: 14, of which 4 were waited for; matrix products, arithmetic and copies ran while one was open for 14% of the time, Pallas kernels for 0%

commit v1 on v0

--- a/solution.py
+++ b/solution.py
@@ -60,7 +60,7 @@
     local_self = jnp.dot(flat, flat.T, precision=lax.Precision.HIGHEST)
     local_earlier = jnp.dot(earlier_flat, earlier_flat.T, precision=lax.Precision.HIGHEST)
     cross_sum, self_sum, earlier_sum = lax.psum(
-        (local_cross, local_self, local_earlier), ("slab", "sub")
+        lax.psum((local_cross, local_self, local_earlier), "sub"), "slab"
     )
     projection = cross_sum / count
     rest = flat - jnp.dot(projection.T, earlier_flat, precision=lax.Precision.HIGHEST)

time: 178 us -> 184 us (1.034)
  blocking collectives: 42.9 us -> 48.8 us
    psum x1 -> x2, blocking collectives: 42.9 us -> 48.8 us  [the longest x1 36.3 us: body(): lax.psum(lax.psum((local_cross, local_self, local_earlier), 'sub'), 'slab')]
  transfers between devices with their start and end apart: 14 -> 14, of which waited for: 4 -> 4; matrix products, arithmetic and copies ran while one was open for 14% -> 13% of each run, Pallas kernels for 0% -> 0%
where the time goes in v1:
time: 184 us; the launch traced here: 183 us
  blocking collectives  48.8 us (27%)
  starting transfers between devices  37.9 us (21%)
  local copies, waits for them, and re-layouts  32.4 us (18%)
  waiting for transfers between devices  28 us (15%)
  other arithmetic  21.6 us (12%)
  matrix products  9.97 us (5%)
  between operations  4.49 us (2%)
    psum x1, blocking collectives, body(): lax.psum(lax.psum((local_cross, local_self, local_earlier), 'sub'), 'slab')  36.3 us
    ppermute x7, starting transfers between devices, padded_2(): lax.ppermute(lax.slice_in_dim(block, block.shape[dim] - width, None, axis...  28.7 us
    ppermute x7, waiting for transfers between devices, padded_2(): lax.ppermute(lax.slice_in_dim(block, block.shape[dim] - width, None, axis...  21.9 us
    reduce_sum x5, other arithmetic, apply_padded(): jnp.sum(coefficients[coupling] * fields[coupling][None], axis=1)  15.2 us
    psum x1, blocking collectives, body(): lax.psum((local_cross, local_self, local_earlier), 'sub')  12.5 us
    ppermute x7, starting transfers between devices, padded_2(): lax.ppermute(lax.slice_in_dim(block, 0, width, axis=dim), axis, backward)  9.21 us
    unnamed x26, local copies, waits for them, and re-layouts  8.24 us
    another operation x18, local copies, waits for them, and re-layouts, body(): basis = jnp.stack(vectors)  8.1 us
  transfers between devices with their start and end apart: 14, of which 4 were waited for; matrix products, arithmetic and copies ran while one was open for 13% of the time, Pallas kernels for 0%

profile of v1, /device:TPU:0, one launch (start us, length us, event | category | flops | bytes accessed | tf_op | source)
XLA Modules:
  0.0 183.1 jit_solution(9244571424164511415)
XLA Ops:
  0.6 1.0 fusion.71
  1.6 1.3 collective-permute-start.1
  2.9 5.5 %collective-permute-start = (f32[6,5,3,128]{3,1,2,0:T(8,128)S(1)}, f32[6,5,3,128]{3,1,2,0:T(8,128)S(1)}, u32[]{:S(2)}, u32[]{:S(2)}) collective-permute-start(f32[6,5,3,128]{3,1,2,0:T(8,128)S(1)} %get-tuple-element.115), channel_id=1, source_target_pairs={{0,4},{4,8},{8,12},{12,16},{16,20},{20,24},{24,28},{1,5},{5,9},{9,... | collective-permute-start | bytes 138248 | tf_op jit(solution)/shard_map/ppermute | solution.py:12
  8.4 2.5 %fusion.55 = (bf16[7,6,6,5,3,128]{5,3,4,2,1,0:T(8,128)(2,1)S(1)}, bf16[7,6,6,5,3,128]{5,3,4,2,1,0:T(8,128)(2,1)S(1)}) fusion(bf16[7,6,6,8,3,128]{5,3,4,2,1,0:T(8,128)(2,1)} %param.4), kind=kLoop, calls=%fused_computation.150 | loop fusion | bytes 3870720 | tf_op jit(solution)/shard_map/slice | solution.py:13
  10.9 1.5 copy.352
  12.4 1.3 collective-permute-start.3
  13.7 1.5 copy.351
  15.2 6.6 %collective-permute-start.2 = (bf16[7,6,6,5,3,128]{5,0,4,3,2,1:T(8,128)(2,1)}, bf16[7,6,6,5,3,128]{5,0,4,3,2,1:T(8,128)(2,1)}, u32[]{:S(2)}, u32[]{:S(2)}) collective-permute-start(bf16[7,6,6,5,3,128]{5,0,4,3,2,1:T(8,128)(2,1)} %copy.351), channel_id=1, source_target_pairs={{0,4},{4,8},{8,12},{12,16},{16,20},{20,24},{24,28},{1,5},{5,9},{9,... | collective-permute-start | bytes 2903048 | tf_op jit(solution)/shard_map/ppermute | solution.py:12
  21.8 2.3 %fusion.39 = f32[30,30]{1,0:T(8,128)S(1)} fusion(f32[30,6,8,3,128]{4,2,3,1,0:T(8,128)S(1)} %copy-done.1), kind=kOutput, calls=%fused_computation.76 | convolution fusion | flops 199065600 | bytes 2215440 | tf_op jit(solution)/shard_map/dot_general | solution.py:61
  24.1 0.7 fusion.72
  24.9 2.6 %copy.340 = f32[30,6,8,3,128]{4,3,2,1,0:T(4,128)} copy(f32[30,6,8,3,128]{4,2,3,1,0:T(8,128)S(1)} %copy-done.1) | data formatting | bytes 4423680 | tf_op args[1]
  30.8 4.5 %reshape.317 = f32[30,18432]{1,0:T(8,128)} reshape(f32[30,6,8,3,128]{4,3,2,1,0:T(4,128)} %copy.340) | data formatting | bytes 4423680 | tf_op jit(solution)/shard_map/reshape | solution.py:57
  35.4 1.3 collective-permute-start.4
  36.7 1.3 collective-permute-start.5
  38.3 3.3 %collective-permute-done.5 = f32[6,18,1,128]{3,1,2,0:T(8,128)S(1)} collective-permute-done((f32[6,18,1,128]{3,1,2,0:T(8,128)S(1)}, f32[6,18,1,128]{3,1,2,0:T(8,128)S(1)}, u32[]{:S(2)}, u32[]{:S(2)}) %collective-permute-start.5) | collective-permute-done | bytes 55328 | tf_op jit(solution)/shard_map/ppermute | solution.py:15
  41.7 1.6 copy.319
  43.3 21.9 %collective-permute-done.2 = bf16[7,6,6,5,3,128]{5,0,4,3,2,1:T(8,128)(2,1)} collective-permute-done((bf16[7,6,6,5,3,128]{5,0,4,3,2,1:T(8,128)(2,1)}, bf16[7,6,6,5,3,128]{5,0,4,3,2,1:T(8,128)(2,1)}, u32[]{:S(2)}, u32[]{:S(2)}) %collective-permute-start.2) | collective-permute-done | bytes 967712 | tf_op jit(solution)/shard_map/ppermute | solution.py:12
  65.2 1.6 copy.318
  66.8 2.9 %pad_maximum_fusion = bf16[7,6,6,18,3,128]{5,3,4,2,1,0:T(8,128)(2,1)S(1)} fusion(bf16[7,6,6,5,3,128]{5,3,4,2,1,0:T(8,128)(2,1)S(1)} %copy.319, bf16[7,6,6,8,3,128]{5,3,4,2,1,0:T(8,128)(2,1)S(1)} %copy-done.2, bf16[7,6,6,5,3,128]{5,3,4,2,1,0:T(8,128)(2,1)S(1)} %copy.318), kind=kLoop, calls=%fused_computation.1 | loop fusion | flops 10450944 | bytes 6967296 | tf_op jit(solution)/shard_map/concatenate | solution.py:16
  69.7 1.1 fusion.4
  70.8 1.1 copy-done
  72.1 0.6 fusion.67
  72.8 1.9 %collective-permute-start.6 = (f32[6,18,1,128]{3,1,2,0:T(8,128)}, f32[6,18,1,128]{3,1,2,0:T(8,128)S(1)}, u32[]{:S(2)}, u32[]{:S(2)}) collective-permute-start(f32[6,18,1,128]{3,1,2,0:T(8,128)} %get-tuple-element.105), channel_id=1, source_target_pairs={{0,1},{1,2},{2,3},{4,5},{5,6},{6,7},{8,9},{9,10},{10,11},{12,13},{... | collective-permute-start | bytes 165896 | tf_op jit(solution)/shard_map/ppermute | solution.py:12
  74.7 1.5 collective-permute-start.7
  76.2 0.7 stack.43
  77.2 1.7 collective-permute-done.7
  79.1 3.5 %fusion.5 = (f32[6,18,3,128]{3,1,2,0:T(8,128)S(1)}, f32[6,18,3,128]{3,1,2,0:T(8,128)S(1)}, f32[6,18,3,128]{3,1,2,0:T(8,128)S(1)}, f32[6,18,3,128]{3,1,2,0:T(8,12...) fusion(f32[6,18,3,128]{3,1,2,0:T(8,128)S(1)} %add_add_fusion.3, ...), kind=kLoop, calls=%fused_computation.42 | loop fusion | flops 4935168 | bytes 5806080 | tf_op jit(solution)/shard_map/reduce_sum | solution.py:40
  82.8 0.7 fusion.65
  83.5 4.9 %collective-permute-start.8 = (f32[6,18,1,128]{3,1,2,0:T(8,128)}, f32[6,18,1,128]{3,1,2,0:T(8,128)S(1)}, u32[]{:S(2)}, u32[]{:S(2)}) collective-permute-start(f32[6,18,1,128]{3,1,2,0:T(8,128)} %get-tuple-element.99), channel_id=1, source_target_pairs={{0,1},{1,2},{2,3},{4,5},{5,6},{6,7},{8,9},{9,10},{10,11},{12,13},{... | collective-permute-start | bytes 165896 | tf_op jit(solution)/shard_map/ppermute | solution.py:12
  88.4 1.3 collective-permute-start.9
  89.8 0.7 stack.44
  90.7 1.0 collective-permute-done.9
  91.9 3.5 %fusion.6 = (f32[6,18,3,128]{3,1,2,0:T(8,128)S(1)}, f32[6,18,3,128]{3,1,2,0:T(8,128)S(1)}, f32[6,18,3,128]{3,1,2,0:T(8,128)S(1)}, f32[6,18,3,128]{3,1,2,0:T(8,12...) fusion(f32[6,18,3,128]{3,1,2,0:T(8,128)S(1)} %add_add_fusion.2, ...), kind=kLoop, calls=%fused_computation.43 | loop fusion | flops 4935168 | bytes 5806080 | tf_op jit(solution)/shard_map/reduce_sum | solution.py:40
  95.7 0.7 fusion.63
  96.4 4.4 %collective-permute-start.10 = (f32[6,18,1,128]{3,1,2,0:T(8,128)}, f32[6,18,1,128]{3,1,2,0:T(8,128)S(1)}, u32[]{:S(2)}, u32[]{:S(2)}) collective-permute-start(f32[6,18,1,128]{3,1,2,0:T(8,128)} %get-tuple-element.93), channel_id=1, source_target_pairs={{0,1},{1,2},{2,3},{4,5},{5,6},{6,7},{8,9},{9,10},{10,11},{12,13},{... | collective-permute-start | bytes 165896 | tf_op jit(solution)/shard_map/ppermute | solution.py:12
  100.8 1.3 collective-permute-start.11
  102.1 0.6 slice_bitcast_fusion.8
  102.8 0.7 stack.45
  103.7 1.0 copy.323
  104.8 3.5 %fusion.7 = (f32[6,18,3,128]{3,1,2,0:T(8,128)S(1)}, f32[6,18,3,128]{3,1,2,0:T(8,128)S(1)}, f32[6,18,3,128]{3,1,2,0:T(8,128)S(1)}, f32[6,18,3,128]{3,1,2,0:T(8,12...) fusion(f32[6,18,3,128]{3,1,2,0:T(8,128)S(1)} %add_add_fusion.1, ...), kind=kLoop, calls=%fused_computation.44 | loop fusion | flops 4935168 | bytes 5806080 | tf_op jit(solution)/shard_map/reduce_sum | solution.py:40
  108.6 0.7 fusion.61
  109.3 4.0 %collective-permute-start.12 = (f32[6,18,1,128]{3,1,2,0:T(8,128)}, f32[6,18,1,128]{3,1,2,0:T(8,128)S(1)}, u32[]{:S(2)}, u32[]{:S(2)}) collective-permute-start(f32[6,18,1,128]{3,1,2,0:T(8,128)} %get-tuple-element.87), channel_id=1, source_target_pairs={{0,1},{1,2},{2,3},{4,5},{5,6},{6,7},{8,9},{9,10},{10,11},{12,13},{... | collective-permute-start | bytes 165896 | tf_op jit(solution)/shard_map/ppermute | solution.py:12
  113.3 1.3 collective-permute-start.13
  114.6 0.6 slice_bitcast_fusion.7
  115.2 0.7 stack.46
  116.1 1.0 copy.324
  117.2 3.5 %fusion.8 = (f32[6,18,3,128]{3,1,2,0:T(8,128)S(1)}, f32[6,18,3,128]{3,1,2,0:T(8,128)S(1)}, f32[6,18,3,128]{3,1,2,0:T(8,128)S(1)}, f32[6,18,3,128]{3,1,2,0:T(8,12...) fusion(f32[6,18,3,128]{3,1,2,0:T(8,128)S(1)} %add_add_fusion, ...), kind=kLoop, calls=%fused_computation.45 | loop fusion | flops 4935168 | bytes 5806080 | tf_op jit(solution)/shard_map/reduce_sum | solution.py:40
  121.0 0.7 stack.41
  121.8 2.2 %fusion.42 = f32[30,6]{0,1:T(8,128)S(1)} fusion(f32[6,6,8,3,128]{4,0,3,2,1:T(8,128)S(1)} %stack.41, f32[30,6,8,3,128]{4,2,3,1,0:T(8,128)S(1)} %copy-done.1), kind=kOutput, calls=%fused_computation.77 | convolution fusion | flops 39813120 | bytes 2654928 | tf_op jit(solution)/shard_map/dot_general | solution.py:59
  124.0 1.4 convolution_bitcast_fusion
  125.5 12.5 %all-reduce.16 = (f32[30,6]{0,1:T(8,128)S(1)}, f32[6,6]{0,1:T(8,128)S(1)}, f32[30,30]{1,0:T(8,128)S(1)}) all-reduce(f32[30,6]{0,1:T(8,128)S(1)} %fusion.42, f32[6,6]{0,1:T(8,128)S(1)} %convolution_bitcast_fusion, f32[30,30]{1,0:T(8,128)S(1)} %fusion.39), channel_id=1, replica_groups=mesh['slab'=8,'sub'=4] {'sub'}, use_global_device_ids=true, to_apply=%region_37.38 | all-reduce | flops 1116 | bytes 8928 | tf_op jit(solution)/shard_map/psum | solution.py:63
  138.0 36.3 %all-reduce.15 = (f32[30,6]{0,1:T(8,128)S(1)}, f32[6,6]{0,1:T(8,128)S(1)}, f32[30,30]{1,0:T(8,128)S(1)}) all-reduce(f32[30,6]{0,1:T(8,128)S(1)} %get-tuple-element.62, f32[6,6]{0,1:T(8,128)S(1)} %get-tuple-element.63, f32[30,30]{1,0:T(8,128)S(1)} %get-tuple-element.64), channel_id=1, replica_groups=mesh['slab'=8,'sub'=4] {'slab'}, use_global_device_ids=true, to_apply=%region_38.39 | all-reduce | flops 1116 | bytes 8928 | tf_op jit(solution)/shard_map/psum | solution.py:62
  174.3 0.1 fusion.45
  174.4 0.1 fusion.47
  174.6 0.1 convolution_add_fusion
  174.8 0.5 cholesky.16
  175.4 0.6 compare_reduce_fusion
  176.1 0.6 fusion.53
  176.7 0.5 custom-call.6
  177.2 0.7 stack.48
  177.9 2.9 %convolution_subtract_fusion = f32[6,18432]{1,0:T(8,128)S(1)} fusion(f32[6,18432]{1,0:T(8,128)S(1)} %stack.48, f32[30,6]{0,1:T(8,128)S(1)} %broadcast_multiply_fusion, f32[30,18432]{1,0:T(8,128)} %reshape.317), kind=kOutput, calls=%fused_computation | convolution fusion | flops 39923712 | bytes 3097296 | tf_op jit(solution)/shard_map/dot_general | solution.py:66
  180.8 0.8 fusion.50
  181.6 0.8 copy.342
  182.4 0.7 copy.343
  (84 shorter events, 3.5 us)
Async XLA Ops:
  1.6 33.7 %collective-permute-start.1 = (f32[6,5,3,128]{3,1,2,0:T(8,128)S(1)}, f32[6,5,3,128]{3,1,2,0:T(8,128)S(1)}, u32[]{:S(2)}, u32[]{:S(2)}) collective-permute-start(f32[6,5,3,128]{3,1,2,0:T(8,128)S(1)} %get-tuple-element.116), channel_id=1, source_target_pairs={{4,0},{8,4},{12,8},{16,12},{20,16},{24,20},{28,24},{5,1},{9,5},{13... | collective-permute-start | bytes 138248 | tf_op jit(solution)/shard_map/ppermute | solution.py:15
  2.9 32.4 %collective-permute-start = (f32[6,5,3,128]{3,1,2,0:T(8,128)S(1)}, f32[6,5,3,128]{3,1,2,0:T(8,128)S(1)}, u32[]{:S(2)}, u32[]{:S(2)}) collective-permute-start(f32[6,5,3,128]{3,1,2,0:T(8,128)S(1)} %get-tuple-element.115), channel_id=1, source_target_pairs={{0,4},{4,8},{8,12},{12,16},{16,20},{20,24},{24,28},{1,5},{5,9},{9,... | collective-permute-start | bytes 138248 | tf_op jit(solution)/shard_map/ppermute | solution.py:12
  12.4 29.3 %collective-permute-start.3 = (bf16[7,6,6,5,3,128]{5,0,4,3,2,1:T(8,128)(2,1)}, bf16[7,6,6,5,3,128]{5,0,4,3,2,1:T(8,128)(2,1)}, u32[]{:S(2)}, u32[]{:S(2)}) collective-permute-start(bf16[7,6,6,5,3,128]{5,0,4,3,2,1:T(8,128)(2,1)} %copy.352), channel_id=1, source_target_pairs={{4,0},{8,4},{12,8},{16,12},{20,16},{24,20},{28,24},{5,1},{9,5},{13... | collective-permute-start | bytes 2903048 | tf_op jit(solution)/shard_map/ppermute | solution.py:15
  13.7 8.1 %copy-start.1 = (f32[30,6,8,3,128]{4,2,3,1,0:T(8,128)S(1)}, f32[30,6,8,3,128]{4,2,3,1,0:T(8,128)}, u32[]{:S(2)}) copy-start(f32[30,6,8,3,128]{4,2,3,1,0:T(8,128)} %param.5) | copy-start | bytes 6635524
  15.2 8.9 %copy-start.9 = (f32[5]{0:T(128)S(1)}, f32[5]{0:T(128)}, u32[]{:S(2)}) copy-start(f32[5]{0:T(128)} %param.7) | copy-start | bytes 64
  15.2 9.6 %copy-start.3 = (f32[6,8,3,128]{3,1,2,0:T(8,128)S(1)}, f32[6,8,3,128]{3,1,2,0:T(8,128)}, u32[]{:S(2)}) copy-start(f32[6,8,3,128]{3,1,2,0:T(8,128)} %param.6) | copy-start | bytes 221188
  15.2 50.0 %collective-permute-start.2 = (bf16[7,6,6,5,3,128]{5,0,4,3,2,1:T(8,128)(2,1)}, bf16[7,6,6,5,3,128]{5,0,4,3,2,1:T(8,128)(2,1)}, u32[]{:S(2)}, u32[]{:S(2)}) collective-permute-start(bf16[7,6,6,5,3,128]{5,0,4,3,2,1:T(8,128)(2,1)} %copy.351), channel_id=1, source_target_pairs={{0,4},{4,8},{8,12},{12,16},{16,20},{20,24},{24,28},{1,5},{5,9},{9,... | collective-permute-start | bytes 2903048 | tf_op jit(solution)/shard_map/ppermute | solution.py:12
  35.4 2.9 %collective-permute-start.4 = (f32[6,18,1,128]{3,1,2,0:T(8,128)S(1)}, f32[6,18,1,128]{3,1,2,0:T(8,128)S(1)}, u32[]{:S(2)}, u32[]{:S(2)}) collective-permute-start(f32[6,18,1,128]{3,1,2,0:T(8,128)S(1)} %get-tuple-element.111), channel_id=1, source_target_pairs={{0,1},{1,2},{2,3},{4,5},{5,6},{6,7},{8,9},{9,10},{10,11},{12,13},{... | collective-permute-start | bytes 165896 | tf_op jit(solution)/shard_map/ppermute | solution.py:12
  36.7 4.9 %collective-permute-start.5 = (f32[6,18,1,128]{3,1,2,0:T(8,128)S(1)}, f32[6,18,1,128]{3,1,2,0:T(8,128)S(1)}, u32[]{:S(2)}, u32[]{:S(2)}) collective-permute-start(f32[6,18,1,128]{3,1,2,0:T(8,128)S(1)} %get-tuple-element.112), channel_id=1, source_target_pairs={{1,0},{2,1},{3,2},{5,4},{6,5},{7,6},{9,8},{10,9},{11,10},{13,12},{... | collective-permute-start | bytes 165896 | tf_op jit(solution)/shard_map/ppermute | solution.py:15
  43.3 23.5 %copy-start.2 = (bf16[7,6,6,8,3,128]{5,3,4,2,1,0:T(8,128)(2,1)S(1)}, bf16[7,6,6,8,3,128]{5,3,4,2,1,0:T(8,128)(2,1)}, u32[]{:S(2)}) copy-start(bf16[7,6,6,8,3,128]{5,3,4,2,1,0:T(8,128)(2,1)} %param.4) | copy-start | bytes 4644868
  69.7 2.2 %copy-start = (bf16[7,6,6,18,3,128]{5,3,4,2,1,0:T(8,128)(2,1)}, bf16[7,6,6,18,3,128]{5,3,4,2,1,0:T(8,128)(2,1)S(1)}, u32[]{:S(2)}) copy-start(bf16[7,6,6,18,3,128]{5,3,4,2,1,0:T(8,128)(2,1)S(1)} %pad_maximum_fusion) | copy-start | bytes 10450948
  72.8 4.4 %collective-permute-start.6 = (f32[6,18,1,128]{3,1,2,0:T(8,128)}, f32[6,18,1,128]{3,1,2,0:T(8,128)S(1)}, u32[]{:S(2)}, u32[]{:S(2)}) collective-permute-start(f32[6,18,1,128]{3,1,2,0:T(8,128)} %get-tuple-element.105), channel_id=1, source_target_pairs={{0,1},{1,2},{2,3},{4,5},{5,6},{6,7},{8,9},{9,10},{10,11},{12,13},{... | collective-permute-start | bytes 165896 | tf_op jit(solution)/shard_map/ppermute | solution.py:12
  74.7 4.3 %collective-permute-start.7 = (f32[6,18,1,128]{3,1,2,0:T(8,128)S(1)}, f32[6,18,1,128]{3,1,2,0:T(8,128)S(1)}, u32[]{:S(2)}, u32[]{:S(2)}) collective-permute-start(f32[6,18,1,128]{3,1,2,0:T(8,128)S(1)} %get-tuple-element.106), channel_id=1, source_target_pairs={{1,0},{2,1},{3,2},{5,4},{6,5},{7,6},{9,8},{10,9},{11,10},{13,12},{... | collective-permute-start | bytes 165896 | tf_op jit(solution)/shard_map/ppermute | solution.py:15
  83.5 7.2 %collective-permute-start.8 = (f32[6,18,1,128]{3,1,2,0:T(8,128)}, f32[6,18,1,128]{3,1,2,0:T(8,128)S(1)}, u32[]{:S(2)}, u32[]{:S(2)}) collective-permute-start(f32[6,18,1,128]{3,1,2,0:T(8,128)} %get-tuple-element.99), channel_id=1, source_target_pairs={{0,1},{1,2},{2,3},{4,5},{5,6},{6,7},{8,9},{9,10},{10,11},{12,13},{... | collective-permute-start | bytes 165896 | tf_op jit(solution)/shard_map/ppermute | solution.py:12
  88.4 3.4 %collective-permute-start.9 = (f32[6,18,1,128]{3,1,2,0:T(8,128)}, f32[6,18,1,128]{3,1,2,0:T(8,128)S(1)}, u32[]{:S(2)}, u32[]{:S(2)}) collective-permute-start(f32[6,18,1,128]{3,1,2,0:T(8,128)} %get-tuple-element.100), channel_id=1, source_target_pairs={{1,0},{2,1},{3,2},{5,4},{6,5},{7,6},{9,8},{10,9},{11,10},{13,12},{... | collective-permute-start | bytes 165896 | tf_op jit(solution)/shard_map/ppermute | solution.py:15
  96.4 8.2 %collective-permute-start.10 = (f32[6,18,1,128]{3,1,2,0:T(8,128)}, f32[6,18,1,128]{3,1,2,0:T(8,128)S(1)}, u32[]{:S(2)}, u32[]{:S(2)}) collective-permute-start(f32[6,18,1,128]{3,1,2,0:T(8,128)} %get-tuple-element.93), channel_id=1, source_target_pairs={{0,1},{1,2},{2,3},{4,5},{5,6},{6,7},{8,9},{9,10},{10,11},{12,13},{... | collective-permute-start | bytes 165896 | tf_op jit(solution)/shard_map/ppermute | solution.py:12
  100.8 3.8 %collective-permute-start.11 = (f32[6,18,1,128]{3,1,2,0:T(8,128)}, f32[6,18,1,128]{3,1,2,0:T(8,128)S(1)}, u32[]{:S(2)}, u32[]{:S(2)}) collective-permute-start(f32[6,18,1,128]{3,1,2,0:T(8,128)} %get-tuple-element.94), channel_id=1, source_target_pairs={{1,0},{2,1},{3,2},{5,4},{6,5},{7,6},{9,8},{10,9},{11,10},{13,12},{... | collective-permute-start | bytes 165896 | tf_op jit(solution)/shard_map/ppermute | solution.py:15
  109.3 7.8 %collective-permute-start.12 = (f32[6,18,1,128]{3,1,2,0:T(8,128)}, f32[6,18,1,128]{3,1,2,0:T(8,128)S(1)}, u32[]{:S(2)}, u32[]{:S(2)}) collective-permute-start(f32[6,18,1,128]{3,1,2,0:T(8,128)} %get-tuple-element.87), channel_id=1, source_target_pairs={{0,1},{1,2},{2,3},{4,5},{5,6},{6,7},{8,9},{9,10},{10,11},{12,13},{... | collective-permute-start | bytes 165896 | tf_op jit(solution)/shard_map/ppermute | solution.py:12
  113.3 3.8 %collective-permute-start.13 = (f32[6,18,1,128]{3,1,2,0:T(8,128)}, f32[6,18,1,128]{3,1,2,0:T(8,128)S(1)}, u32[]{:S(2)}, u32[]{:S(2)}) collective-permute-start(f32[6,18,1,128]{3,1,2,0:T(8,128)} %get-tuple-element.88), channel_id=1, source_target_pairs={{1,0},{2,1},{3,2},{5,4},{6,5},{7,6},{9,8},{10,9},{11,10},{13,12},{... | collective-permute-start | bytes 165896 | tf_op jit(solution)/shard_map/ppermute | solution.py:15
  124.0 53.2 %copy-start.4 = (f32[1,18432]{1,0:T(1,128)S(1)}, f32[1,18432]{1,0:T(1,128)}, u32[]{:S(2)}) copy-start(f32[1,18432]{1,0:T(1,128)} %stack.43) | copy-start | bytes 221188
  124.0 53.2 %copy-start.5 = (f32[1,18432]{1,0:T(1,128)S(1)}, f32[1,18432]{1,0:T(1,128)}, u32[]{:S(2)}) copy-start(f32[1,18432]{1,0:T(1,128)} %stack.44) | copy-start | bytes 221188
  124.0 53.2 %copy-start.6 = (f32[1,18432]{1,0:T(1,128)S(1)}, f32[1,18432]{1,0:T(1,128)}, u32[]{:S(2)}) copy-start(f32[1,18432]{1,0:T(1,128)} %stack.45) | copy-start | bytes 221188
  124.0 53.2 %copy-start.7 = (f32[1,18432]{1,0:T(1,128)S(1)}, f32[1,18432]{1,0:T(1,128)}, u32[]{:S(2)}) copy-start(f32[1,18432]{1,0:T(1,128)} %stack.46) | copy-start | bytes 221188
  174.3 6.5 %copy-start.8 = (f32[30,6]{0,1:T(8,128)}, f32[30,6]{0,1:T(8,128)S(1)}, u32[]{:S(2)}) copy-start(f32[30,6]{0,1:T(8,128)S(1)} %broadcast_multiply_fusion) | copy-start | bytes 2164
